TPU v7x, 512 devices: a whole 4x4x16 slice. The times are simulated.
512 devices in a mesh: gx: 8 (over y, z_hi), gy: 8 (over z_lo), gz: 8 (over x, core).
Axes of the slice: x: 4, y: 4, z: 16 (z_hi: 2, z_lo: 8; z = z_hi * 8 + z_lo), core: 2. Of those that a mesh axis runs over, the one named last changes fastest.
Arguments:
- tokens: bfloat16 [1024, 8192], P('gx', 'gz'), may hold values from -6 to 6
- gate_weight: bfloat16 [8192, 14336], P('gz', ('gx', 'gy')), may hold values from -0.0625 to 0.0625
- up_weight: bfloat16 [8192, 14336], P('gz', ('gx', 'gy')), may hold values from -0.0625 to 0.0625
- down_weight: bfloat16 [14336, 8192], P(('gx', 'gy'), 'gz'), may hold values from -0.046875 to 0.046875
- out_grad: bfloat16 [1024, 8192], P('gx', 'gz'), may hold values from -6 to 6
Outputs:
- output: bfloat16 [1024, 8192], P('gx', 'gz')
- input_grad: bfloat16 [1024, 8192], P('gx', 'gz')
- gate_grad: bfloat16 [8192, 14336], P('gz', ('gx', 'gy'))
- up_grad: bfloat16 [8192, 14336], P('gz', ('gx', 'gy'))
- down_grad: bfloat16 [14336, 8192], P(('gx', 'gy'), 'gz')
All inputs are finite; a program needn't handle non-finite values.
Results may differ from a plain program's by a relative error of at most 0.025.
Values may be sent and summed in bfloat16 or wider, within the bound.
No kernel may reach another device: no remote copies, remote signals or barrier semaphores. Data moves between devices by JAX's collectives and lax.ppermute only.
A program may use at most 64 MiB of HBM per device.

v0:
```python
import jax
import jax.numpy as jnp
from jax import lax
from jax.sharding import Mesh
from jax.sharding import PartitionSpec as P

GX = ("gx_0", "gx_1")
GX_GY = ("gx_0", "gx_1", "gy")


def side_by_side(arrays, axis, dim, along):
    both = jnp.concatenate(arrays, axis=along)
    out, at, finished = (lax.psum_scatter(both, axis, scatter_dimension=dim, tiled=True), 0, [])
    for a in arrays:
        finished.append(lax.slice_in_dim(out, at, at + a.shape[along], axis=along))
        at += a.shape[along]
    return tuple(finished)


def copy_for_each(shard, axis):
    devices = lax.axis_size(axis)
    return lax.all_to_all(
        jnp.broadcast_to(shard[None], (devices, *shard.shape)), axis, 0, 0, tiled=True
    )


def in_order(tiles, dim):
    tiles = jnp.moveaxis(tiles, 0, dim)
    shape = tiles.shape
    return tiles.reshape(*shape[:dim], shape[dim] * shape[dim + 1], *shape[dim + 2 :])


def collect(shard, axis, dim):
    tiles = copy_for_each(shard, axis)
    return in_order(tiles, dim)


def gathered_by_axis(shard, axes, dim):
    if not axes:
        return shard
    nearer = lax.all_gather(shard, axes[-1], axis=dim, tiled=True)
    return gathered_by_axis(nearer, axes[:-1], dim)


def of_everyone(shard, axis):
    everything = copy_for_each(shard, axis)
    return jnp.sum(everything.astype(jnp.float32), axis=0)


def cut_along(shard, dim, devices):
    before, after = (shard.shape[:dim], shard.shape[dim + 1 :])
    return jnp.moveaxis(shard.reshape(*before, devices, -1, *after), dim, 0)


def summed_on_arrival(shard, axis, dim):
    devices = lax.axis_size(axis)
    tiles = lax.all_to_all(cut_along(shard, dim, devices), axis, 0, 0, tiled=True)
    return jnp.sum(tiles.astype(jnp.float32), axis=0)


def sent_together(arrays, axis, dim, along):
    widths = [a.shape[along] for a in arrays]
    both = jnp.concatenate(arrays, axis=along)
    out = lax.all_gather(both, axis, axis=dim, tiled=True)
    return tuple(jnp.split(out, [sum(widths[:k]) for k in range(1, len(widths))], axis=along))


def contract_rows(left, right):
    return lax.dot_general(
        left, right, (((0,), (0,)), ((), ())), preferred_element_type=jnp.float32
    )


def contract_cols(left, right):
    return lax.dot_general(
        left, right, (((1,), (1,)), ((), ())), preferred_element_type=jnp.float32
    )


def activate(gate, upward):
    sigmoid = jax.nn.sigmoid(gate)
    hidden = (gate * sigmoid * upward).astype(jnp.bfloat16)
    return (hidden, sigmoid)


def backward_gates(dhidden, gate, upward, sigmoid):
    dgate = (dhidden * upward * sigmoid * (1.0 + gate * (1.0 - sigmoid))).astype(jnp.bfloat16)
    dupward = (dhidden * gate * sigmoid).astype(jnp.bfloat16)
    return (dgate, dupward)


def body(tokens, gate_weight, up_weight, down_weight, out_grad):
    all_tokens = lax.all_gather(tokens, GX, axis=0, tiled=True)
    gate_part = jnp.dot(all_tokens, gate_weight, preferred_element_type=jnp.float32)
    up_part = jnp.dot(all_tokens, up_weight, preferred_element_type=jnp.float32)
    gate, upward = tuple(
        (
            part.astype(jnp.float32)
            for part in side_by_side(
                (gate_part.astype(jnp.bfloat16), up_part.astype(jnp.bfloat16)), "gz", 0, 1
            )
        )
    )
    hidden_own, sigmoid = activate(gate, upward)
    hidden_all = collect(hidden_own, "gz", 0)
    hidden_mine = lax.all_to_all(hidden_all, GX, split_axis=0, concat_axis=1, tiled=True)
    output_part = jnp.dot(
        hidden_mine, gathered_by_axis(down_weight, GX, 0), preferred_element_type=jnp.float32
    )
    output = (
        of_everyone(output_part.astype(jnp.bfloat16), "gy").astype(jnp.float32).astype(jnp.bfloat16)
    )
    all_grad = lax.all_gather(out_grad, GX, axis=0, tiled=True)
    dhidden_part = contract_cols(all_grad, down_weight)
    dhidden = summed_on_arrival(dhidden_part.astype(jnp.bfloat16), "gz", 0)
    dgate_own, dup_own = backward_gates(dhidden, gate, upward, sigmoid)
    dgate_all, dup_all = sent_together((dgate_own, dup_own), "gz", 0, 1)
    input_part = lax.psum_scatter(
        (contract_cols(dgate_all, gate_weight) + contract_cols(dup_all, up_weight)).astype(
            jnp.bfloat16
        ),
        GX,
        scatter_dimension=0,
        tiled=True,
    )
    input_grad = of_everyone(input_part, "gy").astype(jnp.float32).astype(jnp.bfloat16)
    gate_grad = contract_rows(all_tokens, dgate_all).astype(jnp.bfloat16)
    up_grad = contract_rows(all_tokens, dup_all).astype(jnp.bfloat16)
    down_grad = contract_rows(hidden_all, all_grad).astype(jnp.bfloat16)
    return (output, input_grad, gate_grad, up_grad, down_grad)


def solution(mesh):
    finer = Mesh(
        mesh.devices.reshape(4, 2, mesh.shape["gy"], mesh.shape["gz"]), ("gx_0", "gx_1", "gy", "gz")
    )
    in_specs = (P(GX, "gz"), P("gz", GX_GY), P("gz", GX_GY), P(GX_GY, "gz"), P(GX, "gz"))
    out_specs = (P(GX, "gz"), P(GX, "gz"), P("gz", GX_GY), P("gz", GX_GY), P(GX_GY, "gz"))
    return jax.shard_map(body, mesh=finer, in_specs=in_specs, out_specs=out_specs, check_vma=False)
```

profile of v0, /device:TPU:2, one launch (start us, length us, event | category | flops | bytes accessed | tf_op | source)
XLA Modules:
  0.0 693.5 jit_solution(4162685620083025210)
XLA Ops:
  7.2 0.0 copy-start
  7.2 0.0 all-gather.4.cloned.1.call-start
  7.2 0.7 all-gather.4.cloned.1.call-update
  7.9 0.0 all-gather.8.cloned.1.call-start
  8.0 0.7 all-gather.8.cloned.1.call-update
  8.7 0.0 reduce-scatter.7.cloned.1.call-start
  8.7 123.5 %all-gather.4.cloned.1.call-done = bf16[1024,1024]{1,0:T(8,128)(2,1)} async-done(((bf16[128,1024]{1,0:T(8,128)(2,1)}), bf16[1024,1024]{1,0:T(8,128)(2,1)}) %all-gather.4.cloned.1.call-update) | async-done | bytes 2097168 | tf_op jit(solution)/shard_map/all_gather | solution.py:93
  132.2 0.0 copy-start.3
  132.2 2.6 convolution_convert_fusion.4
  134.8 0.0 copy-done
  134.8 0.0 copy-done.3
  134.8 0.8 convolution_convert_fusion.5
  135.6 0.0 copy-start.2
  135.6 0.1 pad_maximum_fusion
  135.7 1.3 copy.16
  137.0 0.0 reduce-scatter.7.cloned.1.call-update
  137.0 0.0 all-gather.6.cloned.1.call-start
  137.0 0.0 copy-done.2
  137.1 23.9 %all_gather.16 = bf16[448,1024]{1,0:T(8,128)(2,1)} all-gather(bf16[224,1024]{1,0:T(8,128)(2,1)S(1)} %copy-done.2), channel_id=1, replica_groups=mesh['gx_0'=4,'gx_1'=2,'gy'=8,'gz'=8] {'gx_1'}, dimensions={0}, use_global_device_ids=true | all-gather | bytes 1376256 | tf_op jit(solution)/shard_map/all_gather | solution.py:41
  160.9 0.0 all-gather.6.cloned.1.call-update
  161.0 110.2 %all-gather.8.cloned.1.call-done = bf16[1024,1024]{1,0:T(8,128)(2,1)} async-done(((bf16[128,1024]{1,0:T(8,128)(2,1)}), bf16[1024,1024]{1,0:T(8,128)(2,1)}) %all-gather.8.cloned.1.call-update) | async-done | bytes 2097168 | tf_op jit(solution)/shard_map/all_gather | solution.py:113
  271.2 2.4 fusion
  273.6 0.1 copy.27
  273.7 12.8 %all_to_all.36 = bf16[8,128,224]{1,2,0:T(8,128)(2,1)S(1)} all-to-all(bf16[8,128,224]{1,2,0:T(8,128)(2,1)S(1)} %bitcast.34), channel_id=1, replica_groups=mesh['gx_0'=4,'gx_1'=2,'gy'=8,'gz'=8] {'gz'}, dimensions={0} | all-to-all | bytes 917504 | tf_op jit(solution)/shard_map/all_to_all | solution.py:57
  286.5 0.1 convert_reduce_fusion
  286.5 19.3 %reduce-scatter.7.cloned.1.call-done = bf16[128,448]{1,0:T(8,128)(2,1)} async-done(((bf16[1024,448]{1,0:T(8,128)(2,1)}), bf16[128,448]{1,0:T(8,128)(2,1)}) %reduce-scatter.7.cloned.1.call-update) | async-done | bytes 114704
  305.8 1.1 fusion.20
  306.9 0.1 copy.18
  307.0 0.1 copy.19
  307.1 0.1 fusion.13
  307.2 0.1 broadcast_in_dim.6
  307.3 14.9 %all_to_all.37 = bf16[8,128,224]{1,2,0:T(8,128)(2,1)} all-to-all(bf16[8,128,224]{1,2,0:T(8,128)(2,1)S(1)} %broadcast_in_dim.6), channel_id=1, replica_groups=mesh['gx_0'=4,'gx_1'=2,'gy'=8,'gz'=8] {'gz'}, dimensions={0} | all-to-all | bytes 917504 | tf_op jit(solution)/shard_map/all_to_all | solution.py:22
  322.1 14.5 %all-to-all-start.1 = ((bf16[8,128,224]{1,2,0:T(8,128)(2,1)}), bf16[8,128,224]{1,2,0:T(8,128)(2,1)S(1)}, u32[]{:S(2)}, u32[]{:S(2)}) async-start(bf16[8,128,224]{1,2,0:T(8,128)(2,1)} %all_to_all.37), calls=%async_computation.1 | async-start | bytes 917504 | tf_op jit(solution)/shard_map/all_to_all | solution.py:106
  336.6 29.5 %all-gather.6.cloned.1.call-done = bf16[1792,1024]{1,0:T(8,128)(2,1)} async-done(((bf16[448,1024]{1,0:T(8,128)(2,1)}), bf16[1792,1024]{1,0:T(8,128)(2,1)}) %all-gather.6.cloned.1.call-update) | async-done | bytes 3670032 | tf_op jit(solution)/shard_map/all_gather | solution.py:41
  366.1 0.0 all-to-all-done.1
  366.1 2.7 convolution_convert_fusion.6
  368.9 1.6 broadcast_in_dim.7
  370.5 10.0 %all-to-all-start.2 = ((bf16[8,128,1024]{2,1,0:T(8,128)(2,1)}), bf16[8,128,1024]{2,1,0:T(8,128)(2,1)S(1)}, u32[]{:S(2)}, u32[]{:S(2)}) async-start(bf16[8,128,1024]{2,1,0:T(8,128)(2,1)} %broadcast_in_dim.7), calls=%async_computation.2 | async-start | bytes 4194304 | tf_op jit(solution)/shard_map/all_to_all | solution.py:22
  380.5 0.0 reduce-scatter.5.cloned.1.call-start
  380.5 14.3 %all_gather.19 = bf16[1024,448]{0,1:T(8,128)(2,1)S(1)} all-gather(bf16[128,448]{0,1:T(8,128)(2,1)S(1)} %pad_maximum_fusion.1), channel_id=1, replica_groups=mesh['gx_0'=4,'gx_1'=2,'gy'=8,'gz'=8] {'gz'}, dimensions={0}, use_global_device_ids=true | all-gather | bytes 1032192 | tf_op jit(solution)/shard_map/all_gather | solution.py:64
  394.8 0.0 copy-start.1
  394.8 0.8 fusion.8
  395.6 0.3 copy-done.1
  395.8 2.1 add_convert_fusion
  398.0 0.0 reduce-scatter.5.cloned.1.call-update
  398.0 184.5 %reduce-scatter.5.cloned.1.call-done = bf16[128,1024]{1,0:T(8,128)(2,1)} async-done(((bf16[1024,1024]{1,0:T(8,128)(2,1)}), bf16[128,1024]{1,0:T(8,128)(2,1)}) %reduce-scatter.5.cloned.1.call-update) | async-done | bytes 262160 | tf_op jit(solution)/shard_map/reduce_scatter | solution.py:118
  582.5 0.0 all-to-all-done.2
  582.5 2.6 broadcast_in_dim.8
  585.0 4.3 all-to-all-start.4
  589.4 0.0 copy-start.4
  589.4 3.2 fusion.1
  592.6 0.0 copy-done.4
  592.6 0.0 copy-start.5
  592.6 1.4 fusion.2
  594.0 0.2 copy-done.5
  594.2 2.4 convolution_convert_fusion
  596.6 1.1 reduce_sum.33
  597.7 86.6 %all-to-all-done.4 = bf16[8,128,1024]{2,1,0:T(8,128)(2,1)} async-done(((bf16[8,128,1024]{2,1,0:T(8,128)(2,1)}), bf16[8,128,1024]{2,1,0:T(8,128)(2,1)}, u32[]{:S(2)}, u32[]{:S(2)}) %all-to-all-start.4) | async-done | bytes 2097184 | tf_op jit(solution)/shard_map/all_to_all | solution.py:22
  684.3 2.7 reduce_sum.35
  (1 shorter events, 0.0 us)
Async XLA Ops:
  7.2 127.6 %copy-start = (bf16[1024,224]{0,1:T(8,128)(2,1)S(1)}, bf16[1024,224]{0,1:T(8,128)(2,1)}, u32[]{:S(2)}) copy-start(bf16[1024,224]{0,1:T(8,128)(2,1)} %param.6) | copy-start | bytes 1376260
  7.2 125.0 %all-gather.4.cloned.1.call-start = ((), (), s32[]{:S(2)}) async-start(), calls=%async_computation.7 | async-start | bytes 2359296 | tf_op jit(solution)/shard_map/all_gather | solution.py:93
  7.9 263.3 %all-gather.8.cloned.1.call-start = ((), (), s32[]{:S(2)}) async-start(), calls=%async_computation.9 | async-start | bytes 2359296 | tf_op jit(solution)/shard_map/all_gather | solution.py:113
  8.7 297.1 %reduce-scatter.7.cloned.1.call-start = ((), (), s32[]{:S(2)}) async-start(), calls=%async_computation.11 | async-start | bytes 1179648
  132.2 2.6 copy-start.3
  135.6 1.4 copy-start.2
  137.0 229.1 %all-gather.6.cloned.1.call-start = ((), (), s32[]{:S(2)}) async-start(), calls=%async_computation.8 | async-start | bytes 4587520 | tf_op jit(solution)/shard_map/all_gather | solution.py:41
  322.1 44.0 %all-to-all-start.1 = ((bf16[8,128,224]{1,2,0:T(8,128)(2,1)}), bf16[8,128,224]{1,2,0:T(8,128)(2,1)S(1)}, u32[]{:S(2)}, u32[]{:S(2)}) async-start(bf16[8,128,224]{1,2,0:T(8,128)(2,1)} %all_to_all.37), calls=%async_computation.1 | async-start | bytes 917504 | tf_op jit(solution)/shard_map/all_to_all | solution.py:106
  370.5 212.0 %all-to-all-start.2 = ((bf16[8,128,1024]{2,1,0:T(8,128)(2,1)}), bf16[8,128,1024]{2,1,0:T(8,128)(2,1)S(1)}, u32[]{:S(2)}, u32[]{:S(2)}) async-start(bf16[8,128,1024]{2,1,0:T(8,128)(2,1)} %broadcast_in_dim.7), calls=%async_computation.2 | async-start | bytes 4194304 | tf_op jit(solution)/shard_map/all_to_all | solution.py:22
  380.5 202.0 %reduce-scatter.5.cloned.1.call-start = ((), (), s32[]{:S(2)}) async-start(), calls=%async_computation.10 | async-start | bytes 2359296 | tf_op jit(solution)/shard_map/reduce_scatter | solution.py:118
  394.8 1.0 copy-start.1
  585.0 99.2 %all-to-all-start.4 = ((bf16[8,128,1024]{2,1,0:T(8,128)(2,1)}), bf16[8,128,1024]{2,1,0:T(8,128)(2,1)}, u32[]{:S(2)}, u32[]{:S(2)}) async-start(bf16[8,128,1024]{2,1,0:T(8,128)(2,1)} %broadcast_in_dim.8), calls=%async_computation.5 | async-start | bytes 4194304 | tf_op jit(solution)/shard_map/all_to_all | solution.py:22
  589.4 3.2 copy-start.4
  592.6 1.6 copy-start.5
Sparse Core Ops, SparseCore 0:
  11.2 120.9 all-gather.3
  135.4 135.7 all-gather.7
  274.0 31.7 reduce-scatter.6
  307.8 58.3 all-gather.5
  398.1 184.3 reduce-scatter.4
where the time goes:
time: 694 us
  waiting for transfers between devices  555 us (80%)
  blocking collectives  65.8 us (9%)
  starting transfers between devices  29.1 us (4%)
  matrix products  18.3 us (3%)
  between operations  13.9 us (2%)
  local copies, waits for them, and re-layouts  7.4 us (1%)
    reduce_scatter x1, waiting for transfers between devices, body(): lax.psum_scatter((contract_cols(dgate_all, gate_weight) + contract_cols(d...  184 us
    all_gather x1, waiting for transfers between devices, body(): all_tokens = lax.all_gather(tokens, GX, axis=0, tiled=True)  123 us
    all_gather x1, waiting for transfers between devices, body(): all_grad = lax.all_gather(out_grad, GX, axis=0, tiled=True)  110 us
    all_to_all x2, waiting for transfers between devices, copy_for_each(): lax.all_to_all(jnp.broadcast_to(shard[None], (devices, *shard.shape)), ax...  86.6 us
    all_gather x1, waiting for transfers between devices, gathered_by_axis(): nearer = lax.all_gather(shard, axes[-1], axis=dim, tiled=True)  29.5 us
    all_gather x1, blocking collectives, gathered_by_axis(): nearer = lax.all_gather(shard, axes[-1], axis=dim, tiled=True)  23.9 us
    unnamed x6, waiting for transfers between devices  20.7 us
    all_to_all x1, blocking collectives, copy_for_each(): lax.all_to_all(jnp.broadcast_to(shard[None], (devices, *shard.shape)), ax...  14.9 us
  transfers between devices with their start and end apart: 8, of which 6 were waited for; matrix products, arithmetic and copies ran while one was open for 3% of the time, Pallas kernels for 0%

commit v1 on v0

--- a/solution.py
+++ b/solution.py
@@ -90,7 +90,9 @@
 
 
 def body(tokens, gate_weight, up_weight, down_weight, out_grad):
-    all_tokens = lax.all_gather(tokens, GX, axis=0, tiled=True)
+    all_tokens = jnp.concatenate(
+        lax.all_to_all(jnp.stack([tokens] * lax.axis_size(GX)), GX, 0, 0), axis=0
+    )
     gate_part = jnp.dot(all_tokens, gate_weight, preferred_element_type=jnp.float32)
     up_part = jnp.dot(all_tokens, up_weight, preferred_element_type=jnp.float32)
     gate, upward = tuple(

time: 694 us -> 658 us (0.948)
  waiting for transfers between devices: 555 us -> 443 us
  blocking collectives: 65.8 us -> 122 us
  starting transfers between devices: 29.1 us -> 47 us
    all_gather x1 -> x0, waiting for transfers between devices: 123 us -> none  [body(): all_tokens = lax.all_gather(tokens, GX, axis=0, tiled=True)]
    all_gather x1, waiting for transfers between devices: 110 us -> 17.6 us  [body(): all_grad = lax.all_gather(out_grad, GX, axis=0, tiled=True)]
    all_to_all x0 -> x1, waiting for transfers between devices: none -> 56.7 us  [body(): lax.all_to_all(jnp.stack([tokens] * lax.axis_size(GX)), GX, 0, 0)]
    all_gather x1, blocking collectives: 23.9 us -> 80.3 us  [gathered_by_axis(): nearer = lax.all_gather(shard, axes[-1], axis=dim, tiled=True)]
    unnamed x6 -> x5, waiting for transfers between devices: 20.7 us -> 67.8 us
    all_to_all x0 -> x1, starting transfers between devices: none -> 17.9 us  [body(): lax.all_to_all(jnp.stack([tokens] * lax.axis_size(GX)), GX, 0, 0)]
where the time goes in v1:
time: 658 us; the launch traced here: 657 us
  waiting for transfers between devices  443 us (67%)
  blocking collectives  122 us (19%)
  starting transfers between devices  47 us (7%)
  matrix products  16.6 us (3%)
  between operations  13.9 us (2%)
  local copies, waits for them, and re-layouts  10.5 us (2%)
    reduce_scatter x1, waiting for transfers between devices, body(): lax.psum_scatter((contract_cols(dgate_all, gate_weight) + contract_cols(d...  184 us
    all_to_all x2, waiting for transfers between devices, copy_for_each(): lax.all_to_all(jnp.broadcast_to(shard[None], (devices, *shard.shape)), ax...  86.6 us
    all_gather x1, blocking collectives, gathered_by_axis(): nearer = lax.all_gather(shard, axes[-1], axis=dim, tiled=True)  80.3 us
    unnamed x5, waiting for transfers between devices  67.8 us
    all_to_all x1, waiting for transfers between devices, body(): lax.all_to_all(jnp.stack([tokens] * lax.axis_size(GX)), GX, 0, 0)  56.7 us
    all_gather x1, waiting for transfers between devices, gathered_by_axis(): nearer = lax.all_gather(shard, axes[-1], axis=dim, tiled=True)  29.6 us
    all_to_all x1, starting transfers between devices, body(): lax.all_to_all(jnp.stack([tokens] * lax.axis_size(GX)), GX, 0, 0)  17.9 us
    all_gather x1, waiting for transfers between devices, body(): all_grad = lax.all_gather(out_grad, GX, axis=0, tiled=True)  17.6 us
  transfers between devices with their start and end apart: 8, of which 6 were waited for; matrix products, arithmetic and copies ran while one was open for 3% of the time, Pallas kernels for 0%

profile of v1, /device:TPU:2, one launch (start us, length us, event | category | flops | bytes accessed | tf_op | source)
XLA Modules:
  0.0 656.9 jit_solution(8767794135737963194)
XLA Ops:
  7.2 0.0 copy-start
  7.2 2.6 stack.2
  9.8 0.0 copy-start.3
  9.8 17.9 %all-to-all-start = ((bf16[8,128,1024]{2,1,0:T(8,128)(2,1)}), bf16[8,128,1024]{2,1,0:T(8,128)(2,1)S(1)}, u32[]{:S(2)}, u32[]{:S(2)}) async-start(bf16[8,128,1024]{2,1,0:T(8,128)(2,1)} %stack.2), calls=%async_computation | async-start | bytes 4194304 | tf_op jit(solution)/shard_map/all_to_all | solution.py:94
  27.6 0.0 all-gather.5.cloned.1.call-start
  27.7 0.7 all-gather.5.cloned.1.call-update
  28.4 0.0 reduce-scatter.7.cloned.1.call-start
  28.4 56.7 %all-to-all-done = bf16[8,128,1024]{2,1,0:T(8,128)(2,1)S(1)} async-done(((bf16[8,128,1024]{2,1,0:T(8,128)(2,1)}), bf16[8,128,1024]{2,1,0:T(8,128)(2,1)S(1)}, u32[]{:S(2)}, u32[]{:S(2)}) %all-to-all-start) | async-done | bytes 2097184 | tf_op jit(solution)/shard_map/all_to_all | solution.py:94
  85.1 0.0 copy-start.1
  85.1 0.0 copy-done.3
  85.1 0.8 convolution_convert_fusion.4
  85.9 0.5 copy-done.1
  86.4 0.0 copy-done
  86.4 0.8 convolution_convert_fusion.5
  87.2 0.0 copy-start.5
  87.2 0.1 pad_maximum_fusion
  87.3 1.3 copy.16
  88.6 0.0 reduce-scatter.7.cloned.1.call-update
  88.6 0.0 all-gather.3.cloned.1.call-start
  88.7 0.0 copy-done.5
  88.7 80.3 %all_gather.12 = bf16[448,1024]{1,0:T(8,128)(2,1)} all-gather(bf16[224,1024]{1,0:T(8,128)(2,1)S(1)} %copy-done.5), channel_id=1, replica_groups=mesh['gx_0'=4,'gx_1'=2,'gy'=8,'gz'=8] {'gx_1'}, dimensions={0}, use_global_device_ids=true | all-gather | bytes 1376256 | tf_op jit(solution)/shard_map/all_gather | solution.py:41
  169.0 0.0 all-gather.3.cloned.1.call-update
  169.0 17.6 %all-gather.5.cloned.1.call-done = bf16[1024,1024]{1,0:T(8,128)(2,1)} async-done(((bf16[128,1024]{1,0:T(8,128)(2,1)}), bf16[1024,1024]{1,0:T(8,128)(2,1)}) %all-gather.5.cloned.1.call-update) | async-done | bytes 2097168 | tf_op jit(solution)/shard_map/all_gather | solution.py:115
  186.6 2.4 fusion
  189.0 0.1 copy.27
  189.1 12.8 %all_to_all.41 = bf16[8,128,224]{1,2,0:T(8,128)(2,1)S(1)} all-to-all(bf16[8,128,224]{1,2,0:T(8,128)(2,1)S(1)} %bitcast.39), channel_id=1, replica_groups=mesh['gx_0'=4,'gx_1'=2,'gy'=8,'gz'=8] {'gz'}, dimensions={0} | all-to-all | bytes 917504 | tf_op jit(solution)/shard_map/all_to_all | solution.py:57
  201.8 0.1 convert_reduce_fusion
  201.9 67.1 %reduce-scatter.7.cloned.1.call-done = bf16[128,448]{1,0:T(8,128)(2,1)} async-done(((bf16[1024,448]{1,0:T(8,128)(2,1)}), bf16[128,448]{1,0:T(8,128)(2,1)}) %reduce-scatter.7.cloned.1.call-update) | async-done | bytes 114704
  269.0 1.1 fusion.20
  270.0 0.1 copy.18
  270.1 0.1 copy.19
  270.3 0.1 fusion.13
  270.4 0.1 broadcast_in_dim.6
  270.4 14.8 %all_to_all.42 = bf16[8,128,224]{1,2,0:T(8,128)(2,1)} all-to-all(bf16[8,128,224]{1,2,0:T(8,128)(2,1)S(1)} %broadcast_in_dim.6), channel_id=1, replica_groups=mesh['gx_0'=4,'gx_1'=2,'gy'=8,'gz'=8] {'gz'}, dimensions={0} | all-to-all | bytes 917504 | tf_op jit(solution)/shard_map/all_to_all | solution.py:22
  285.3 14.6 %all-to-all-start.2 = ((bf16[8,128,224]{1,2,0:T(8,128)(2,1)}), bf16[8,128,224]{1,2,0:T(8,128)(2,1)S(1)}, u32[]{:S(2)}, u32[]{:S(2)}) async-start(bf16[8,128,224]{1,2,0:T(8,128)(2,1)} %all_to_all.42), calls=%async_computation.2 | async-start | bytes 917504 | tf_op jit(solution)/shard_map/all_to_all | solution.py:108
  299.9 29.6 %all-gather.3.cloned.1.call-done = bf16[1792,1024]{1,0:T(8,128)(2,1)} async-done(((bf16[448,1024]{1,0:T(8,128)(2,1)}), bf16[1792,1024]{1,0:T(8,128)(2,1)}) %all-gather.3.cloned.1.call-update) | async-done | bytes 3670032 | tf_op jit(solution)/shard_map/all_gather | solution.py:41
  329.5 0.0 all-to-all-done.2
  329.5 2.7 convolution_convert_fusion.6
  332.2 1.6 broadcast_in_dim.7
  333.9 10.0 %all-to-all-start.3 = ((bf16[8,128,1024]{2,1,0:T(8,128)(2,1)}), bf16[8,128,1024]{2,1,0:T(8,128)(2,1)S(1)}, u32[]{:S(2)}, u32[]{:S(2)}) async-start(bf16[8,128,1024]{2,1,0:T(8,128)(2,1)} %broadcast_in_dim.7), calls=%async_computation.3 | async-start | bytes 4194304 | tf_op jit(solution)/shard_map/all_to_all | solution.py:22
  343.9 0.0 reduce-scatter.5.cloned.1.call-start
  343.9 14.3 %all_gather.15 = bf16[1024,448]{0,1:T(8,128)(2,1)S(1)} all-gather(bf16[128,448]{0,1:T(8,128)(2,1)S(1)} %pad_maximum_fusion.1), channel_id=1, replica_groups=mesh['gx_0'=4,'gx_1'=2,'gy'=8,'gz'=8] {'gz'}, dimensions={0}, use_global_device_ids=true | all-gather | bytes 1032192 | tf_op jit(solution)/shard_map/all_gather | solution.py:64
  358.2 0.0 copy-start.4
  358.2 0.7 fusion.8
  358.9 0.3 copy-done.4
  359.2 2.1 add_convert_fusion
  361.3 0.0 reduce-scatter.5.cloned.1.call-update
  361.4 184.4 %reduce-scatter.5.cloned.1.call-done = bf16[128,1024]{1,0:T(8,128)(2,1)} async-done(((bf16[1024,1024]{1,0:T(8,128)(2,1)}), bf16[128,1024]{1,0:T(8,128)(2,1)}) %reduce-scatter.5.cloned.1.call-update) | async-done | bytes 262160 | tf_op jit(solution)/shard_map/reduce_scatter | solution.py:120
  545.8 0.0 all-to-all-done.3
  545.8 2.6 broadcast_in_dim.8
  548.4 4.3 all-to-all-start.5
  552.8 0.0 copy-start.2
  552.8 3.2 fusion.1
  555.9 0.0 copy-done.2
  555.9 0.0 copy-start.6
  555.9 1.4 fusion.2
  557.3 0.2 copy-done.6
  557.5 2.4 convolution_convert_fusion
  560.0 1.1 reduce_sum.33
  561.0 86.6 %all-to-all-done.5 = bf16[8,128,1024]{2,1,0:T(8,128)(2,1)} async-done(((bf16[8,128,1024]{2,1,0:T(8,128)(2,1)}), bf16[8,128,1024]{2,1,0:T(8,128)(2,1)}, u32[]{:S(2)}, u32[]{:S(2)}) %all-to-all-start.5) | async-done | bytes 2097184 | tf_op jit(solution)/shard_map/all_to_all | solution.py:22
  647.6 2.7 reduce_sum.35
  (1 shorter events, 0.0 us)
Async XLA Ops:
  7.2 79.3 %copy-start = (bf16[1024,224]{0,1:T(8,128)(2,1)S(1)}, bf16[1024,224]{0,1:T(8,128)(2,1)}, u32[]{:S(2)}) copy-start(bf16[1024,224]{0,1:T(8,128)(2,1)} %param.6) | copy-start | bytes 1376260
  9.8 75.3 %copy-start.3 = (bf16[1024,224]{0,1:T(8,128)(2,1)S(1)}, bf16[1024,224]{0,1:T(8,128)(2,1)}, u32[]{:S(2)}) copy-start(bf16[1024,224]{0,1:T(8,128)(2,1)} %param.7) | copy-start | bytes 1376260
  9.8 75.3 %all-to-all-start = ((bf16[8,128,1024]{2,1,0:T(8,128)(2,1)}), bf16[8,128,1024]{2,1,0:T(8,128)(2,1)S(1)}, u32[]{:S(2)}, u32[]{:S(2)}) async-start(bf16[8,128,1024]{2,1,0:T(8,128)(2,1)} %stack.2), calls=%async_computation | async-start | bytes 4194304 | tf_op jit(solution)/shard_map/all_to_all | solution.py:94
  27.6 158.9 %all-gather.5.cloned.1.call-start = ((), (), s32[]{:S(2)}) async-start(), calls=%async_computation.9 | async-start | bytes 2359296 | tf_op jit(solution)/shard_map/all_gather | solution.py:115
  28.4 240.6 %reduce-scatter.7.cloned.1.call-start = ((), (), s32[]{:S(2)}) async-start(), calls=%async_computation.11 | async-start | bytes 1179648
  85.1 1.3 copy-start.1
  87.2 1.4 copy-start.5
  88.6 240.9 %all-gather.3.cloned.1.call-start = ((), (), s32[]{:S(2)}) async-start(), calls=%async_computation.8 | async-start | bytes 4587520 | tf_op jit(solution)/shard_map/all_gather | solution.py:41
  285.3 44.3 %all-to-all-start.2 = ((bf16[8,128,224]{1,2,0:T(8,128)(2,1)}), bf16[8,128,224]{1,2,0:T(8,128)(2,1)S(1)}, u32[]{:S(2)}, u32[]{:S(2)}) async-start(bf16[8,128,224]{1,2,0:T(8,128)(2,1)} %all_to_all.42), calls=%async_computation.2 | async-start | bytes 917504 | tf_op jit(solution)/shard_map/all_to_all | solution.py:108
  333.9 211.9 %all-to-all-start.3 = ((bf16[8,128,1024]{2,1,0:T(8,128)(2,1)}), bf16[8,128,1024]{2,1,0:T(8,128)(2,1)S(1)}, u32[]{:S(2)}, u32[]{:S(2)}) async-start(bf16[8,128,1024]{2,1,0:T(8,128)(2,1)} %broadcast_in_dim.7), calls=%async_computation.3 | async-start | bytes 4194304 | tf_op jit(solution)/shard_map/all_to_all | solution.py:22
  343.9 202.0 %reduce-scatter.5.cloned.1.call-start = ((), (), s32[]{:S(2)}) async-start(), calls=%async_computation.10 | async-start | bytes 2359296 | tf_op jit(solution)/shard_map/reduce_scatter | solution.py:120
  358.2 1.0 copy-start.4
  548.4 99.2 %all-to-all-start.5 = ((bf16[8,128,1024]{2,1,0:T(8,128)(2,1)}), bf16[8,128,1024]{2,1,0:T(8,128)(2,1)}, u32[]{:S(2)}, u32[]{:S(2)}) async-start(bf16[8,128,1024]{2,1,0:T(8,128)(2,1)} %broadcast_in_dim.8), calls=%async_computation.6 | async-start | bytes 4194304 | tf_op jit(solution)/shard_map/all_to_all | solution.py:22
  552.8 3.2 copy-start.2
  555.9 1.6 copy-start.6
Sparse Core Ops, SparseCore 0:
  31.6 154.8 all-gather.4
  189.4 79.5 reduce-scatter.6
  271.1 58.3 all-gather.2
  361.5 184.2 reduce-scatter.4
